TPU v7x, 32 devices: a whole 2x2x4 slice. The times are simulated.
32 devices in a mesh: row: 4 (over x, core), col: 8 (over z, y).
Axes of the slice: x: 2, y: 2, z: 4, core: 2. Of those that a mesh axis runs over, the one named last changes fastest.
Arguments:
- vectors: float32 [8192, 1024], P('row', 'col'), may hold values from -6 to 6
- reflectors: float32 [4, 32, 256, 128], P('row', 'col'), may hold values from -0.375 to 0.375
- wy_factors: float32 [4, 32, 128, 128], P('row', 'col'), may hold values from -1 to 3, as said below
- block_slots: int32 [4, 4, 4], P('row'), may hold values from 0 to 31, as said below
- offsets: int32 [4, 4, 3], P('row'), may hold values from 0 to 1792
Outputs:
- transformed: float32 [8192, 1024], P('row', 'col')
Inputs may be any that keep to these rules, and one draw needn't show every extreme that they name: `wy_factors`: upper triangular; diagonal entries between 1.2 and 2.8. `block_slots`: the entries of one row group are distinct; slot k of every group lies on the col index k // 4. The border entry of the last row group is not read.
All inputs are finite; a program needn't handle non-finite values.
Results may differ from a plain program's by a relative error of at most 0.00026.
Values sent between devices are 32-bit elements; how exact they have to be, the bound alone decides.
No kernel may reach another device: no remote copies, remote signals or barrier semaphores. Data moves between devices by JAX's collectives and lax.ppermute only.
A program may use at most 64 MiB of HBM per device.

v0:
```python
import jax
import jax.numpy as jnp
from jax import lax
from jax.sharding import PartitionSpec as P


def spread(block, axis, source):
    block = jnp.where(lax.axis_index(axis) == source, block, jnp.zeros_like(block))
    return lax.psum(block, axis)


def shifted(block, axis, distance):
    devices = range(lax.axis_size(axis))
    route = [(i - distance, i) for i in devices if i - distance in devices]
    return lax.ppermute(block, axis, route)


def reflect(block, basis, factor):
    best = lax.Precision.HIGHEST
    coeffs = jnp.dot(basis.T, block, precision=best, preferred_element_type=jnp.float32)
    scaled = jnp.dot(factor, coeffs, precision=best, preferred_element_type=jnp.float32)
    return block - jnp.dot(basis, scaled, precision=best, preferred_element_type=jnp.float32)


def fetch_block(block_slots, reflectors, wy_factors, step_no, block_no):
    hold_count = reflectors.shape[1]
    slot_id = block_slots[0, step_no, block_no]
    local_slot = slot_id % hold_count
    root_col = slot_id // hold_count
    parcel = (
        lax.dynamic_index_in_dim(reflectors[0], local_slot, 0, False),
        lax.dynamic_index_in_dim(wy_factors[0], local_slot, 0, False),
    )
    return (spread(parcel[0], "col", root_col), spread(parcel[1], "col", root_col))


def advance(
    current, incoming, beneath, step_no, group_index, group_total_count, bases, factors, offsets
):
    edge_rows = beneath.shape[0]
    total_rows = current.shape[0]
    inner_count = offsets.shape[2]
    head = jnp.where(group_index > 0, incoming, current[:edge_rows])
    current = lax.dynamic_update_slice_in_dim(current, head, 0, 0)
    step_bases = lax.dynamic_index_in_dim(bases, step_no, 0, False)
    step_factors = lax.dynamic_index_in_dim(factors, step_no, 0, False)
    step_offsets = lax.dynamic_index_in_dim(offsets[0], step_no, 0, False)
    for block_no in range(inner_count):
        start = step_offsets[block_no]
        block = lax.dynamic_slice_in_dim(current, start, 2 * edge_rows, 0)
        block = reflect(block, step_bases[block_no], step_factors[block_no])
        current = lax.dynamic_update_slice_in_dim(current, block, start, 0)
    bottom = current[total_rows - edge_rows :]
    joined = reflect(
        jnp.concatenate([bottom, beneath], 0), step_bases[inner_count], step_factors[inner_count]
    )
    has_below = group_index < group_total_count - 1
    tail = jnp.where(has_below, joined[:edge_rows], bottom)
    current = lax.dynamic_update_slice_in_dim(current, tail, total_rows - edge_rows, 0)
    return (current, joined[edge_rows:])


def per_device(vectors, reflectors, wy_factors, block_slots, offsets):
    group_total_count = lax.axis_size("row")
    group_index = lax.axis_index("row")
    step_count = offsets.shape[1]
    inner_count = offsets.shape[2]
    edge_rows = reflectors.shape[3]
    column_count = vectors.shape[1]
    base_list = []
    factor_list = []
    for step_no in range(step_count):
        for block_no in range(inner_count + 1):
            basis, factor = fetch_block(block_slots, reflectors, wy_factors, step_no, block_no)
            base_list.append(basis)
            factor_list.append(factor)
    bases = jnp.stack(base_list).reshape((step_count, inner_count + 1) + base_list[0].shape)
    factors = jnp.stack(factor_list).reshape((step_count, inner_count + 1) + factor_list[0].shape)
    empty_rows = jnp.zeros((edge_rows, column_count), jnp.float32)
    current = vectors

    def wave_tick(tick_no, carry):
        current, incoming = carry
        beneath = shifted(current[:edge_rows], "row", -1)
        time_lag = tick_no - group_index
        step_now = time_lag // 2
        active = (time_lag >= 0) & (time_lag % 2 == 0) & (step_now < step_count)
        step_safe = jnp.clip(step_now, 0, step_count - 1)
        current, outgoing = lax.cond(
            active,
            lambda operands: advance(
                operands[0],
                operands[1],
                beneath,
                step_safe,
                group_index,
                group_total_count,
                bases,
                factors,
                offsets,
            ),
            lambda operands: (operands[0], jnp.zeros_like(operands[1])),
            (current, incoming),
        )
        incoming = shifted(outgoing, "row", 1)
        return (current, incoming)

    current, incoming = lax.fori_loop(
        0, group_total_count + 2 * step_count - 2, wave_tick, (current, empty_rows)
    )
    return current


def solution(mesh):
    in_specs = (
        P("row", "col"),
        P("row", "col", None, None),
        P("row", "col", None, None),
        P("row", None, None),
        P("row", None, None),
    )
    out_specs = P("row", "col")
    return jax.shard_map(
        per_device, mesh=mesh, in_specs=in_specs, out_specs=out_specs, check_vma=False
    )
```

profile of v0, /device:TPU:3, one launch (start us, length us, event | category | flops | bytes accessed | tf_op | source)
XLA Modules:
  0.0 467.4 jit_solution(14436373289902219683)
XLA Ops:
  51.6 144.5 %all-reduce.3.cloned.1.call-done = (f32[1,256,128]{2,1,0:T(8,128)}, f32[1,256,128]{2,1,0:T(8,128)}, f32[1,256,128]{2,1,0:T(8,128)}, f32[1,256,128]{2,1,0:T(8,128...) async-done(((f32[1,256,128]{2,1,0:T(8,128)}, ...) | async-done | bytes 3145744 | tf_op jit(solution)/shard_map/psum | solution.py:9
  210.9 248.8 %while.20 = (s32[]{:T(128)}, f32[2048,128]{1,0:T(8,128)S(1)}, f32[128,128]{1,0:T(8,128)S(1)}, s32[]{:T(128)}, s32[1,4,3]{1,0,2:T(1,128)S(1)}, /*index=5*/f32[4,4...) while((s32[]{:T(128)}, f32[2048,128]{1,0:T(8,128)S(1)}, ...), condition=%wide.region_35.36_spmd, body=%wide.region_32.35_spmd.sunk | while | flops 503545888 | bytes 6030164 | solution.py:108
  210.9 2.7 collective-permute-start
  214.5 1.3 collective-permute-start.1
  215.8 2.4 collective-permute-done.1
  218.2 4.9 %collective-permute-start = (f32[128,128]{1,0:T(8,128)S(1)}, f32[128,128]{1,0:T(8,128)S(1)}, u32[]{:S(2)}, u32[]{:S(2)}) collective-permute-start(f32[128,128]{1,0:T(8,128)S(1)} %slice.171), channel_id=1, source_target_pairs={{8,0},{16,8},{24,16},{9,1},{17,9},{25,17},{10,2},{18,10},{26,18},{... | collective-permute-start | bytes 196616 | tf_op jit(solution)/shard_map/while/body/eval_jaxpr/ppermute | solution.py:15
  224.0 1.3 collective-permute-start.1
  225.2 14.6 %collective-permute-done.1 = f32[128,128]{1,0:T(8,128)S(1)} collective-permute-done((f32[128,128]{1,0:T(8,128)S(1)}, f32[128,128]{1,0:T(8,128)S(1)}, u32[]{:S(2)}, u32[]{:S(2)}) %collective-permute-start.1) | collective-permute-done | bytes 65568 | tf_op jit(solution)/shard_map/while/body/eval_jaxpr/ppermute | solution.py:15
  239.9 20.7 %collective-permute-start = (f32[128,128]{1,0:T(8,128)S(1)}, f32[128,128]{1,0:T(8,128)S(1)}, u32[]{:S(2)}, u32[]{:S(2)}) collective-permute-start(f32[128,128]{1,0:T(8,128)S(1)} %slice.171), channel_id=1, source_target_pairs={{8,0},{16,8},{24,16},{9,1},{17,9},{25,17},{10,2},{18,10},{26,18},{... | collective-permute-start | bytes 196616 | tf_op jit(solution)/shard_map/while/body/eval_jaxpr/ppermute | solution.py:15
  262.8 18.6 %collective-permute-done.1 = f32[128,128]{1,0:T(8,128)S(1)} collective-permute-done((f32[128,128]{1,0:T(8,128)S(1)}, f32[128,128]{1,0:T(8,128)S(1)}, u32[]{:S(2)}, u32[]{:S(2)}) %collective-permute-start.1) | collective-permute-done | bytes 65568 | tf_op jit(solution)/shard_map/while/body/eval_jaxpr/ppermute | solution.py:15
  281.3 4.8 %collective-permute-start = (f32[128,128]{1,0:T(8,128)S(1)}, f32[128,128]{1,0:T(8,128)S(1)}, u32[]{:S(2)}, u32[]{:S(2)}) collective-permute-start(f32[128,128]{1,0:T(8,128)S(1)} %slice.171), channel_id=1, source_target_pairs={{8,0},{16,8},{24,16},{9,1},{17,9},{25,17},{10,2},{18,10},{26,18},{... | collective-permute-start | bytes 196616 | tf_op jit(solution)/shard_map/while/body/eval_jaxpr/ppermute | solution.py:15
  287.1 16.2 %conditional.2 = (f32[2048,128]{1,0:T(8,128)S(1)}, f32[128,128]{1,0:T(8,128)S(1)}) conditional(s32[]{:T(128)} %convert_element_type.11, f32[2048,128]{1,0:T(8,128)S(1)} %get-tuple-element.402, (s32[]{:T(128)}, f32[2048,128]{1,0:T(8,128)S(1)}, f32[128,128]{1,0:T(8,128)S(1)}, s32[]{:T(128)}, s32[1,4,3]{1,0,2:T(1,128)S(1)}, ...), branch_computations={%region_33.33_spmd, %region_34.34_spmd} | conditional | flops 503545856 | bytes 5374306 | solution.py:89
  303.3 1.3 collective-permute-start.1
  304.6 1.8 collective-permute-done.1
  306.4 5.1 %collective-permute-start = (f32[128,128]{1,0:T(8,128)S(1)}, f32[128,128]{1,0:T(8,128)S(1)}, u32[]{:S(2)}, u32[]{:S(2)}) collective-permute-start(f32[128,128]{1,0:T(8,128)S(1)} %slice.171), channel_id=1, source_target_pairs={{8,0},{16,8},{24,16},{9,1},{17,9},{25,17},{10,2},{18,10},{26,18},{... | collective-permute-start | bytes 196616 | tf_op jit(solution)/shard_map/while/body/eval_jaxpr/ppermute | solution.py:15
  313.7 18.6 %collective-permute-done.1 = f32[128,128]{1,0:T(8,128)S(1)} collective-permute-done((f32[128,128]{1,0:T(8,128)S(1)}, f32[128,128]{1,0:T(8,128)S(1)}, u32[]{:S(2)}, u32[]{:S(2)}) %collective-permute-start.1) | collective-permute-done | bytes 65568 | tf_op jit(solution)/shard_map/while/body/eval_jaxpr/ppermute | solution.py:15
  332.3 4.8 %collective-permute-start = (f32[128,128]{1,0:T(8,128)S(1)}, f32[128,128]{1,0:T(8,128)S(1)}, u32[]{:S(2)}, u32[]{:S(2)}) collective-permute-start(f32[128,128]{1,0:T(8,128)S(1)} %slice.171), channel_id=1, source_target_pairs={{8,0},{16,8},{24,16},{9,1},{17,9},{25,17},{10,2},{18,10},{26,18},{... | collective-permute-start | bytes 196616 | tf_op jit(solution)/shard_map/while/body/eval_jaxpr/ppermute | solution.py:15
  338.0 16.1 %conditional.2 = (f32[2048,128]{1,0:T(8,128)S(1)}, f32[128,128]{1,0:T(8,128)S(1)}) conditional(s32[]{:T(128)} %convert_element_type.11, f32[2048,128]{1,0:T(8,128)S(1)} %get-tuple-element.402, (s32[]{:T(128)}, f32[2048,128]{1,0:T(8,128)S(1)}, f32[128,128]{1,0:T(8,128)S(1)}, s32[]{:T(128)}, s32[1,4,3]{1,0,2:T(1,128)S(1)}, ...), branch_computations={%region_33.33_spmd, %region_34.34_spmd} | conditional | flops 503545856 | bytes 5374306 | solution.py:89
  354.1 1.3 collective-permute-start.1
  355.4 1.8 collective-permute-done.1
  357.2 5.4 %collective-permute-start = (f32[128,128]{1,0:T(8,128)S(1)}, f32[128,128]{1,0:T(8,128)S(1)}, u32[]{:S(2)}, u32[]{:S(2)}) collective-permute-start(f32[128,128]{1,0:T(8,128)S(1)} %slice.171), channel_id=1, source_target_pairs={{8,0},{16,8},{24,16},{9,1},{17,9},{25,17},{10,2},{18,10},{26,18},{... | collective-permute-start | bytes 196616 | tf_op jit(solution)/shard_map/while/body/eval_jaxpr/ppermute | solution.py:15
  364.8 18.6 %collective-permute-done.1 = f32[128,128]{1,0:T(8,128)S(1)} collective-permute-done((f32[128,128]{1,0:T(8,128)S(1)}, f32[128,128]{1,0:T(8,128)S(1)}, u32[]{:S(2)}, u32[]{:S(2)}) %collective-permute-start.1) | collective-permute-done | bytes 65568 | tf_op jit(solution)/shard_map/while/body/eval_jaxpr/ppermute | solution.py:15
  383.4 4.8 %collective-permute-start = (f32[128,128]{1,0:T(8,128)S(1)}, f32[128,128]{1,0:T(8,128)S(1)}, u32[]{:S(2)}, u32[]{:S(2)}) collective-permute-start(f32[128,128]{1,0:T(8,128)S(1)} %slice.171), channel_id=1, source_target_pairs={{8,0},{16,8},{24,16},{9,1},{17,9},{25,17},{10,2},{18,10},{26,18},{... | collective-permute-start | bytes 196616 | tf_op jit(solution)/shard_map/while/body/eval_jaxpr/ppermute | solution.py:15
  389.1 16.2 %conditional.2 = (f32[2048,128]{1,0:T(8,128)S(1)}, f32[128,128]{1,0:T(8,128)S(1)}) conditional(s32[]{:T(128)} %convert_element_type.11, f32[2048,128]{1,0:T(8,128)S(1)} %get-tuple-element.402, (s32[]{:T(128)}, f32[2048,128]{1,0:T(8,128)S(1)}, f32[128,128]{1,0:T(8,128)S(1)}, s32[]{:T(128)}, s32[1,4,3]{1,0,2:T(1,128)S(1)}, ...), branch_computations={%region_33.33_spmd, %region_34.34_spmd} | conditional | flops 503545856 | bytes 5374306 | solution.py:89
  405.3 1.3 collective-permute-start.1
  406.6 1.8 collective-permute-done.1
  408.5 5.4 %collective-permute-start = (f32[128,128]{1,0:T(8,128)S(1)}, f32[128,128]{1,0:T(8,128)S(1)}, u32[]{:S(2)}, u32[]{:S(2)}) collective-permute-start(f32[128,128]{1,0:T(8,128)S(1)} %slice.171), channel_id=1, source_target_pairs={{8,0},{16,8},{24,16},{9,1},{17,9},{25,17},{10,2},{18,10},{26,18},{... | collective-permute-start | bytes 196616 | tf_op jit(solution)/shard_map/while/body/eval_jaxpr/ppermute | solution.py:15
  416.1 18.6 %collective-permute-done.1 = f32[128,128]{1,0:T(8,128)S(1)} collective-permute-done((f32[128,128]{1,0:T(8,128)S(1)}, f32[128,128]{1,0:T(8,128)S(1)}, u32[]{:S(2)}, u32[]{:S(2)}) %collective-permute-start.1) | collective-permute-done | bytes 65568 | tf_op jit(solution)/shard_map/while/body/eval_jaxpr/ppermute | solution.py:15
  434.7 4.8 %collective-permute-start = (f32[128,128]{1,0:T(8,128)S(1)}, f32[128,128]{1,0:T(8,128)S(1)}, u32[]{:S(2)}, u32[]{:S(2)}) collective-permute-start(f32[128,128]{1,0:T(8,128)S(1)} %slice.171), channel_id=1, source_target_pairs={{8,0},{16,8},{24,16},{9,1},{17,9},{25,17},{10,2},{18,10},{26,18},{... | collective-permute-start | bytes 196616 | tf_op jit(solution)/shard_map/while/body/eval_jaxpr/ppermute | solution.py:15
  440.4 16.1 %conditional.2 = (f32[2048,128]{1,0:T(8,128)S(1)}, f32[128,128]{1,0:T(8,128)S(1)}) conditional(s32[]{:T(128)} %convert_element_type.11, f32[2048,128]{1,0:T(8,128)S(1)} %get-tuple-element.402, (s32[]{:T(128)}, f32[2048,128]{1,0:T(8,128)S(1)}, f32[128,128]{1,0:T(8,128)S(1)}, s32[]{:T(128)}, s32[1,4,3]{1,0,2:T(1,128)S(1)}, ...), branch_computations={%region_33.33_spmd, %region_34.34_spmd} | conditional | flops 503545856 | bytes 5374306 | solution.py:89
  456.5 1.3 collective-permute-start.1
  457.8 1.8 collective-permute-done.1
  (200 shorter events, 76.2 us)
Async XLA Ops:
  6.5 42.2 %copy-start.2 = (f32[1,4,256,128]{3,2,1,0:T(8,128)S(1)}, f32[1,4,256,128]{3,2,1,0:T(8,128)}, u32[]{:S(2)}) copy-start(f32[1,4,256,128]{3,2,1,0:T(8,128)} %param.10) | copy-start | bytes 1572868
  6.5 41.4 %copy-start.3 = (f32[1,4,128,128]{3,2,1,0:T(8,128)S(1)}, f32[1,4,128,128]{3,2,1,0:T(8,128)}, u32[]{:S(2)}) copy-start(f32[1,4,128,128]{3,2,1,0:T(8,128)} %param.11) | copy-start | bytes 786436
  6.5 189.5 %all-reduce.3.cloned.1.call-start = ((), (), s32[]{:S(2)}) async-start(), calls=%async_computation | async-start | bytes 6291456 | tf_op jit(solution)/shard_map/psum | solution.py:9
  196.1 13.2 %copy-start.20 = (f32[1,128,128]{2,1,0:T(8,128)S(1)}, f32[1,128,128]{2,1,0:T(8,128)}, u32[]{:S(2)}) copy-start(f32[1,128,128]{2,1,0:T(8,128)} %get-tuple-element.284) | copy-start | bytes 196612
  196.1 13.2 %copy-start.19 = (f32[1,256,128]{2,1,0:T(8,128)S(1)}, f32[1,256,128]{2,1,0:T(8,128)}, u32[]{:S(2)}) copy-start(f32[1,256,128]{2,1,0:T(8,128)} %get-tuple-element.254) | copy-start | bytes 393220
  196.1 13.3 %copy-start.18 = (f32[1,256,128]{2,1,0:T(8,128)S(1)}, f32[1,256,128]{2,1,0:T(8,128)}, u32[]{:S(2)}) copy-start(f32[1,256,128]{2,1,0:T(8,128)} %get-tuple-element.255) | copy-start | bytes 393220
  196.1 13.3 %copy-start.17 = (f32[1,256,128]{2,1,0:T(8,128)S(1)}, f32[1,256,128]{2,1,0:T(8,128)}, u32[]{:S(2)}) copy-start(f32[1,256,128]{2,1,0:T(8,128)} %get-tuple-element.256) | copy-start | bytes 393220
  196.1 13.3 %copy-start.16 = (f32[1,256,128]{2,1,0:T(8,128)S(1)}, f32[1,256,128]{2,1,0:T(8,128)}, u32[]{:S(2)}) copy-start(f32[1,256,128]{2,1,0:T(8,128)} %get-tuple-element.257) | copy-start | bytes 393220
  196.1 13.3 %copy-start.15 = (f32[1,256,128]{2,1,0:T(8,128)S(1)}, f32[1,256,128]{2,1,0:T(8,128)}, u32[]{:S(2)}) copy-start(f32[1,256,128]{2,1,0:T(8,128)} %get-tuple-element.258) | copy-start | bytes 393220
  196.1 13.4 %copy-start.14 = (f32[1,256,128]{2,1,0:T(8,128)S(1)}, f32[1,256,128]{2,1,0:T(8,128)}, u32[]{:S(2)}) copy-start(f32[1,256,128]{2,1,0:T(8,128)} %get-tuple-element.259) | copy-start | bytes 393220
  196.1 13.4 %copy-start.13 = (f32[1,256,128]{2,1,0:T(8,128)S(1)}, f32[1,256,128]{2,1,0:T(8,128)}, u32[]{:S(2)}) copy-start(f32[1,256,128]{2,1,0:T(8,128)} %get-tuple-element.260) | copy-start | bytes 393220
  196.1 13.4 %copy-start.12 = (f32[1,256,128]{2,1,0:T(8,128)S(1)}, f32[1,256,128]{2,1,0:T(8,128)}, u32[]{:S(2)}) copy-start(f32[1,256,128]{2,1,0:T(8,128)} %get-tuple-element.261) | copy-start | bytes 393220
  210.9 3.6 collective-permute-start
  214.5 3.7 collective-permute-start.1
  218.2 5.8 %collective-permute-start = (f32[128,128]{1,0:T(8,128)S(1)}, f32[128,128]{1,0:T(8,128)S(1)}, u32[]{:S(2)}, u32[]{:S(2)}) collective-permute-start(f32[128,128]{1,0:T(8,128)S(1)} %slice.171), channel_id=1, source_target_pairs={{8,0},{16,8},{24,16},{9,1},{17,9},{25,17},{10,2},{18,10},{26,18},{... | collective-permute-start | bytes 196616 | tf_op jit(solution)/shard_map/while/body/eval_jaxpr/ppermute | solution.py:15
  224.0 15.9 %collective-permute-start.1 = (f32[128,128]{1,0:T(8,128)S(1)}, f32[128,128]{1,0:T(8,128)S(1)}, u32[]{:S(2)}, u32[]{:S(2)}) collective-permute-start(f32[128,128]{1,0:T(8,128)S(1)} %get-tuple-element.384), channel_id=1, source_target_pairs={{0,8},{8,16},{16,24},{1,9},{9,17},{17,25},{2,10},{10,18},{18,26},{... | collective-permute-start | bytes 196616 | tf_op jit(solution)/shard_map/while/body/eval_jaxpr/ppermute | solution.py:15
  239.9 21.6 %collective-permute-start = (f32[128,128]{1,0:T(8,128)S(1)}, f32[128,128]{1,0:T(8,128)S(1)}, u32[]{:S(2)}, u32[]{:S(2)}) collective-permute-start(f32[128,128]{1,0:T(8,128)S(1)} %slice.171), channel_id=1, source_target_pairs={{8,0},{16,8},{24,16},{9,1},{17,9},{25,17},{10,2},{18,10},{26,18},{... | collective-permute-start | bytes 196616 | tf_op jit(solution)/shard_map/while/body/eval_jaxpr/ppermute | solution.py:15
  261.5 19.9 %collective-permute-start.1 = (f32[128,128]{1,0:T(8,128)S(1)}, f32[128,128]{1,0:T(8,128)S(1)}, u32[]{:S(2)}, u32[]{:S(2)}) collective-permute-start(f32[128,128]{1,0:T(8,128)S(1)} %get-tuple-element.384), channel_id=1, source_target_pairs={{0,8},{8,16},{16,24},{1,9},{9,17},{17,25},{2,10},{10,18},{18,26},{... | collective-permute-start | bytes 196616 | tf_op jit(solution)/shard_map/while/body/eval_jaxpr/ppermute | solution.py:15
  281.3 5.7 %collective-permute-start = (f32[128,128]{1,0:T(8,128)S(1)}, f32[128,128]{1,0:T(8,128)S(1)}, u32[]{:S(2)}, u32[]{:S(2)}) collective-permute-start(f32[128,128]{1,0:T(8,128)S(1)} %slice.171), channel_id=1, source_target_pairs={{8,0},{16,8},{24,16},{9,1},{17,9},{25,17},{10,2},{18,10},{26,18},{... | collective-permute-start | bytes 196616 | tf_op jit(solution)/shard_map/while/body/eval_jaxpr/ppermute | solution.py:15
  303.3 3.1 collective-permute-start.1
  306.4 6.0 %collective-permute-start = (f32[128,128]{1,0:T(8,128)S(1)}, f32[128,128]{1,0:T(8,128)S(1)}, u32[]{:S(2)}, u32[]{:S(2)}) collective-permute-start(f32[128,128]{1,0:T(8,128)S(1)} %slice.171), channel_id=1, source_target_pairs={{8,0},{16,8},{24,16},{9,1},{17,9},{25,17},{10,2},{18,10},{26,18},{... | collective-permute-start | bytes 196616 | tf_op jit(solution)/shard_map/while/body/eval_jaxpr/ppermute | solution.py:15
  312.4 19.9 %collective-permute-start.1 = (f32[128,128]{1,0:T(8,128)S(1)}, f32[128,128]{1,0:T(8,128)S(1)}, u32[]{:S(2)}, u32[]{:S(2)}) collective-permute-start(f32[128,128]{1,0:T(8,128)S(1)} %get-tuple-element.384), channel_id=1, source_target_pairs={{0,8},{8,16},{16,24},{1,9},{9,17},{17,25},{2,10},{10,18},{18,26},{... | collective-permute-start | bytes 196616 | tf_op jit(solution)/shard_map/while/body/eval_jaxpr/ppermute | solution.py:15
  332.3 5.7 %collective-permute-start = (f32[128,128]{1,0:T(8,128)S(1)}, f32[128,128]{1,0:T(8,128)S(1)}, u32[]{:S(2)}, u32[]{:S(2)}) collective-permute-start(f32[128,128]{1,0:T(8,128)S(1)} %slice.171), channel_id=1, source_target_pairs={{8,0},{16,8},{24,16},{9,1},{17,9},{25,17},{10,2},{18,10},{26,18},{... | collective-permute-start | bytes 196616 | tf_op jit(solution)/shard_map/while/body/eval_jaxpr/ppermute | solution.py:15
  354.1 3.1 collective-permute-start.1
  357.2 6.3 %collective-permute-start = (f32[128,128]{1,0:T(8,128)S(1)}, f32[128,128]{1,0:T(8,128)S(1)}, u32[]{:S(2)}, u32[]{:S(2)}) collective-permute-start(f32[128,128]{1,0:T(8,128)S(1)} %slice.171), channel_id=1, source_target_pairs={{8,0},{16,8},{24,16},{9,1},{17,9},{25,17},{10,2},{18,10},{26,18},{... | collective-permute-start | bytes 196616 | tf_op jit(solution)/shard_map/while/body/eval_jaxpr/ppermute | solution.py:15
  363.6 19.9 %collective-permute-start.1 = (f32[128,128]{1,0:T(8,128)S(1)}, f32[128,128]{1,0:T(8,128)S(1)}, u32[]{:S(2)}, u32[]{:S(2)}) collective-permute-start(f32[128,128]{1,0:T(8,128)S(1)} %get-tuple-element.384), channel_id=1, source_target_pairs={{0,8},{8,16},{16,24},{1,9},{9,17},{17,25},{2,10},{10,18},{18,26},{... | collective-permute-start | bytes 196616 | tf_op jit(solution)/shard_map/while/body/eval_jaxpr/ppermute | solution.py:15
  383.4 5.7 %collective-permute-start = (f32[128,128]{1,0:T(8,128)S(1)}, f32[128,128]{1,0:T(8,128)S(1)}, u32[]{:S(2)}, u32[]{:S(2)}) collective-permute-start(f32[128,128]{1,0:T(8,128)S(1)} %slice.171), channel_id=1, source_target_pairs={{8,0},{16,8},{24,16},{9,1},{17,9},{25,17},{10,2},{18,10},{26,18},{... | collective-permute-start | bytes 196616 | tf_op jit(solution)/shard_map/while/body/eval_jaxpr/ppermute | solution.py:15
  405.3 3.1 collective-permute-start.1
  408.5 6.3 %collective-permute-start = (f32[128,128]{1,0:T(8,128)S(1)}, f32[128,128]{1,0:T(8,128)S(1)}, u32[]{:S(2)}, u32[]{:S(2)}) collective-permute-start(f32[128,128]{1,0:T(8,128)S(1)} %slice.171), channel_id=1, source_target_pairs={{8,0},{16,8},{24,16},{9,1},{17,9},{25,17},{10,2},{18,10},{26,18},{... | collective-permute-start | bytes 196616 | tf_op jit(solution)/shard_map/while/body/eval_jaxpr/ppermute | solution.py:15
  414.8 19.9 %collective-permute-start.1 = (f32[128,128]{1,0:T(8,128)S(1)}, f32[128,128]{1,0:T(8,128)S(1)}, u32[]{:S(2)}, u32[]{:S(2)}) collective-permute-start(f32[128,128]{1,0:T(8,128)S(1)} %get-tuple-element.384), channel_id=1, source_target_pairs={{0,8},{8,16},{16,24},{1,9},{9,17},{17,25},{2,10},{10,18},{18,26},{... | collective-permute-start | bytes 196616 | tf_op jit(solution)/shard_map/while/body/eval_jaxpr/ppermute | solution.py:15
  434.7 5.7 %collective-permute-start = (f32[128,128]{1,0:T(8,128)S(1)}, f32[128,128]{1,0:T(8,128)S(1)}, u32[]{:S(2)}, u32[]{:S(2)}) collective-permute-start(f32[128,128]{1,0:T(8,128)S(1)} %slice.171), channel_id=1, source_target_pairs={{8,0},{16,8},{24,16},{9,1},{17,9},{25,17},{10,2},{18,10},{26,18},{... | collective-permute-start | bytes 196616 | tf_op jit(solution)/shard_map/while/body/eval_jaxpr/ppermute | solution.py:15
  456.5 3.1 collective-permute-start.1
  (13 other events, 69.4 us)
Sparse Core Ops, SparseCore 0:
  51.7 144.3 all-reduce.2
where the time goes:
time: 470 us; the launch traced here: 467 us
  waiting for transfers between devices  252 us (54%)
  starting transfers between devices  76.4 us (16%)
  between operations  53.7 us (11%)
  local copies, waits for them, and re-layouts  31.5 us (7%)
  matrix products  27.3 us (6%)
  loops' own time  23.2 us (5%)
    psum x1, waiting for transfers between devices, spread(): return lax.psum(block, axis)  144 us
    ppermute x20, waiting for transfers between devices, shifted(): return lax.ppermute(block, axis, route)  107 us
    ppermute x20, starting transfers between devices, shifted(): return lax.ppermute(block, axis, route)  76.4 us
    another operation x10, loops' own time, wave_tick(): lax.cond(active, lambda operands: advance(operands[0], operands[1], benea...  22.5 us
    dot_general x16, matrix products, reflect(): jnp.dot(factor, coeffs, precision=best, preferred_element_type=jnp.float32)  16.8 us
    unnamed x78, local copies, waits for them, and re-layouts  16.1 us
    dynamic_update_slice x12, local copies, waits for them, and re-layouts, advance(): current = lax.dynamic_update_slice_in_dim(current, block, start, 0)  11.9 us
  transfers between devices with their start and end apart: 21, of which 21 were waited for; matrix products, arithmetic and copies ran while one was open for 0% of the time, Pallas kernels for 0%

commit v1 on v0

--- a/solution.py
+++ b/solution.py
@@ -6,7 +6,7 @@
 
 def spread(block, axis, source):
     block = jnp.where(lax.axis_index(axis) == source, block, jnp.zeros_like(block))
-    return lax.psum(block, axis)
+    return jnp.sum(jax.lax.all_gather(block, axis), axis=0)
 
 
 def shifted(block, axis, distance):

time: 470 us -> 977 us (2.08)
  blocking collectives: 0 us -> 422 us
  waiting for transfers between devices: 252 us -> 318 us
  other arithmetic: 3.81 us -> 27.4 us
    all_gather x0 -> x16, blocking collectives: none -> 422 us  [spread(): return jnp.sum(jax.lax.all_gather(block, axis), axis=0)]
    all_gather x0 -> x16, waiting for transfers between devices: none -> 202 us  [spread(): return jnp.sum(jax.lax.all_gather(block, axis), axis=0)]
    psum x1 -> x0, waiting for transfers between devices: 144 us -> none  [spread(): return lax.psum(block, axis)]
    reduce_sum x0 -> x32, other arithmetic: none -> 25 us  [spread(): return jnp.sum(jax.lax.all_gather(block, axis), axis=0)]
  transfers between devices with their start and end apart: 21 -> 36, of which waited for: 21 -> 26; matrix products, arithmetic and copies ran while one was open for 0% -> 3% of each run, Pallas kernels for 0% -> 0%
where the time goes in v1:
time: 977 us; the launch traced here: 974 us
  blocking collectives  422 us (43%)
  waiting for transfers between devices  318 us (33%)
  starting transfers between devices  78.7 us (8%)
  between operations  53.9 us (6%)
  other arithmetic  27.4 us (3%)
  matrix products  27.3 us (3%)
  local copies, waits for them, and re-layouts  23.8 us (2%)
  loops' own time  23.7 us (2%)
    all_gather x16, blocking collectives, spread(): return jnp.sum(jax.lax.all_gather(block, axis), axis=0)  422 us
    all_gather x16, waiting for transfers between devices, spread(): return jnp.sum(jax.lax.all_gather(block, axis), axis=0)  202 us
    ppermute x20, waiting for transfers between devices, shifted(): return lax.ppermute(block, axis, route)  108 us
    ppermute x20, starting transfers between devices, shifted(): return lax.ppermute(block, axis, route)  78.1 us
    reduce_sum x32, other arithmetic, spread(): return jnp.sum(jax.lax.all_gather(block, axis), axis=0)  25 us
    another operation x10, loops' own time, wave_tick(): lax.cond(active, lambda operands: advance(operands[0], operands[1], benea...  23 us
  transfers between devices with their start and end apart: 36, of which 26 were waited for; matrix products, arithmetic and copies ran while one was open for 3% of the time, Pallas kernels for 0%

profile of v1, /device:TPU:3, one launch (start us, length us, event | category | flops | bytes accessed | tf_op | source)
XLA Modules:
  0.0 974.2 jit_solution(5201008511222446966)
XLA Ops:
  59.5 26.2 %all-gather.16 = f32[8,1,128,128]{3,2,1,0:T(8,128)S(1)} all-gather(f32[1,1,128,128]{3,2,1,0:T(8,128)S(1)} %get-tuple-element.289), channel_id=18, replica_groups=mesh['row'=4,'col'=8] {'col'}, dimensions={0}, use_global_device_ids=true | all-gather | bytes 589824 | tf_op jit(solution)/shard_map/all_gather | solution.py:9
  85.7 27.4 %all-gather.17 = f32[8,1,128,128]{3,2,1,0:T(8,128)S(1)} all-gather(f32[1,1,128,128]{3,2,1,0:T(8,128)S(1)} %get-tuple-element.288), channel_id=19, replica_groups=mesh['row'=4,'col'=8] {'col'}, dimensions={0}, use_global_device_ids=true | all-gather | bytes 589824 | tf_op jit(solution)/shard_map/all_gather | solution.py:9
  113.1 26.3 %all-gather.18 = f32[8,1,128,128]{3,2,1,0:T(8,128)S(1)} all-gather(f32[1,1,128,128]{3,2,1,0:T(8,128)S(1)} %get-tuple-element.287), channel_id=20, replica_groups=mesh['row'=4,'col'=8] {'col'}, dimensions={0}, use_global_device_ids=true | all-gather | bytes 589824 | tf_op jit(solution)/shard_map/all_gather | solution.py:9
  139.5 26.0 %all-gather.19 = f32[8,1,128,128]{3,2,1,0:T(8,128)S(1)} all-gather(f32[1,1,128,128]{3,2,1,0:T(8,128)S(1)} %get-tuple-element.286), channel_id=21, replica_groups=mesh['row'=4,'col'=8] {'col'}, dimensions={0}, use_global_device_ids=true | all-gather | bytes 589824 | tf_op jit(solution)/shard_map/all_gather | solution.py:9
  165.5 26.2 %all-gather.20 = f32[8,1,128,128]{3,2,1,0:T(8,128)S(1)} all-gather(f32[1,1,128,128]{3,2,1,0:T(8,128)S(1)} %get-tuple-element.285), channel_id=22, replica_groups=mesh['row'=4,'col'=8] {'col'}, dimensions={0}, use_global_device_ids=true | all-gather | bytes 589824 | tf_op jit(solution)/shard_map/all_gather | solution.py:9
  191.8 26.2 %all-gather.21 = f32[8,1,128,128]{3,2,1,0:T(8,128)S(1)} all-gather(f32[1,1,128,128]{3,2,1,0:T(8,128)S(1)} %get-tuple-element.284), channel_id=23, replica_groups=mesh['row'=4,'col'=8] {'col'}, dimensions={0}, use_global_device_ids=true | all-gather | bytes 589824 | tf_op jit(solution)/shard_map/all_gather | solution.py:9
  218.0 27.0 %all-gather.22 = f32[8,1,128,128]{3,2,1,0:T(8,128)S(1)} all-gather(f32[1,1,128,128]{3,2,1,0:T(8,128)S(1)} %get-tuple-element.282), channel_id=24, replica_groups=mesh['row'=4,'col'=8] {'col'}, dimensions={0}, use_global_device_ids=true | all-gather | bytes 589824 | tf_op jit(solution)/shard_map/all_gather | solution.py:9
  245.1 25.5 %all-gather.23 = f32[8,1,128,128]{3,2,1,0:T(8,128)S(1)} all-gather(f32[1,1,128,128]{3,2,1,0:T(8,128)S(1)} %get-tuple-element.281), channel_id=25, replica_groups=mesh['row'=4,'col'=8] {'col'}, dimensions={0}, use_global_device_ids=true | all-gather | bytes 589824 | tf_op jit(solution)/shard_map/all_gather | solution.py:9
  270.5 26.3 %all-gather.24 = f32[8,1,128,128]{3,2,1,0:T(8,128)S(1)} all-gather(f32[1,1,128,128]{3,2,1,0:T(8,128)S(1)} %get-tuple-element.280), channel_id=26, replica_groups=mesh['row'=4,'col'=8] {'col'}, dimensions={0}, use_global_device_ids=true | all-gather | bytes 589824 | tf_op jit(solution)/shard_map/all_gather | solution.py:9
  296.9 26.3 %all-gather.25 = f32[8,1,128,128]{3,2,1,0:T(8,128)S(1)} all-gather(f32[1,1,128,128]{3,2,1,0:T(8,128)S(1)} %get-tuple-element.279), channel_id=27, replica_groups=mesh['row'=4,'col'=8] {'col'}, dimensions={0}, use_global_device_ids=true | all-gather | bytes 589824 | tf_op jit(solution)/shard_map/all_gather | solution.py:9
  323.2 26.0 %all-gather.26 = f32[8,1,128,128]{3,2,1,0:T(8,128)S(1)} all-gather(f32[1,1,128,128]{3,2,1,0:T(8,128)S(1)} %get-tuple-element.278), channel_id=28, replica_groups=mesh['row'=4,'col'=8] {'col'}, dimensions={0}, use_global_device_ids=true | all-gather | bytes 589824 | tf_op jit(solution)/shard_map/all_gather | solution.py:9
  349.2 26.4 %all-gather.27 = f32[8,1,128,128]{3,2,1,0:T(8,128)S(1)} all-gather(f32[1,1,128,128]{3,2,1,0:T(8,128)S(1)} %get-tuple-element.277), channel_id=29, replica_groups=mesh['row'=4,'col'=8] {'col'}, dimensions={0}, use_global_device_ids=true | all-gather | bytes 589824 | tf_op jit(solution)/shard_map/all_gather | solution.py:9
  375.6 26.3 %all-gather.28 = f32[8,1,128,128]{3,2,1,0:T(8,128)S(1)} all-gather(f32[1,1,128,128]{3,2,1,0:T(8,128)S(1)} %get-tuple-element.276), channel_id=30, replica_groups=mesh['row'=4,'col'=8] {'col'}, dimensions={0}, use_global_device_ids=true | all-gather | bytes 589824 | tf_op jit(solution)/shard_map/all_gather | solution.py:9
  402.0 26.5 %all-gather.29 = f32[8,1,128,128]{3,2,1,0:T(8,128)S(1)} all-gather(f32[1,1,128,128]{3,2,1,0:T(8,128)S(1)} %get-tuple-element.275), channel_id=31, replica_groups=mesh['row'=4,'col'=8] {'col'}, dimensions={0}, use_global_device_ids=true | all-gather | bytes 589824 | tf_op jit(solution)/shard_map/all_gather | solution.py:9
  428.5 27.3 %all-gather.30 = f32[8,1,128,128]{3,2,1,0:T(8,128)S(1)} all-gather(f32[1,1,128,128]{3,2,1,0:T(8,128)S(1)} %get-tuple-element.283), channel_id=32, replica_groups=mesh['row'=4,'col'=8] {'col'}, dimensions={0}, use_global_device_ids=true | all-gather | bytes 589824 | tf_op jit(solution)/shard_map/all_gather | solution.py:9
  455.8 26.1 %all-gather.31 = f32[8,1,128,128]{3,2,1,0:T(8,128)S(1)} all-gather(f32[1,1,128,128]{3,2,1,0:T(8,128)S(1)} %get-tuple-element.274), channel_id=33, replica_groups=mesh['row'=4,'col'=8] {'col'}, dimensions={0}, use_global_device_ids=true | all-gather | bytes 589824 | tf_op jit(solution)/shard_map/all_gather | solution.py:9
  508.7 39.4 %all-gather.71.cloned.1.call-done = f32[8,1,256,128]{3,2,1,0:T(8,128)} async-done(((f32[1,1,256,128]{3,2,1,0:T(8,128)}), f32[8,1,256,128]{3,2,1,0:T(8,128)}) %all-gather.71.cloned.1.call-update) | async-done | bytes 1048592 | tf_op jit(solution)/shard_map/all_gather | solution.py:9
  550.1 40.7 %all-gather.73.cloned.1.call-done = f32[8,1,256,128]{3,2,1,0:T(8,128)} async-done(((f32[1,1,256,128]{3,2,1,0:T(8,128)}), f32[8,1,256,128]{3,2,1,0:T(8,128)}) %all-gather.73.cloned.1.call-update) | async-done | bytes 1048592 | tf_op jit(solution)/shard_map/all_gather | solution.py:9
  592.7 39.1 %all-gather.75.cloned.1.call-done = f32[8,1,256,128]{3,2,1,0:T(8,128)} async-done(((f32[1,1,256,128]{3,2,1,0:T(8,128)}), f32[8,1,256,128]{3,2,1,0:T(8,128)}) %all-gather.75.cloned.1.call-update) | async-done | bytes 1048592 | tf_op jit(solution)/shard_map/all_gather | solution.py:9
  633.7 39.1 %all-gather.77.cloned.1.call-done = f32[8,1,256,128]{3,2,1,0:T(8,128)} async-done(((f32[1,1,256,128]{3,2,1,0:T(8,128)}), f32[8,1,256,128]{3,2,1,0:T(8,128)}) %all-gather.77.cloned.1.call-update) | async-done | bytes 1048592 | tf_op jit(solution)/shard_map/all_gather | solution.py:9
  680.3 33.5 %all-gather.79.cloned.1.call-done = f32[8,1,256,128]{3,2,1,0:T(8,128)} async-done(((f32[1,1,256,128]{3,2,1,0:T(8,128)}), f32[8,1,256,128]{3,2,1,0:T(8,128)}) %all-gather.79.cloned.1.call-update) | async-done | bytes 1048592 | tf_op jit(solution)/shard_map/all_gather | solution.py:9
  715.1 251.6 %while.20 = (s32[]{:T(128)}, f32[2048,128]{1,0:T(8,128)S(1)}, f32[128,128]{1,0:T(8,128)S(1)}, s32[]{:T(128)}, s32[1,4,3]{1,0,2:T(1,128)S(1)}, /*index=5*/f32[4,4...) while((s32[]{:T(128)}, f32[2048,128]{1,0:T(8,128)S(1)}, ...), condition=%wide.region_35.36_spmd, body=%wide.region_32.35_spmd.sunk | while | flops 503545888 | bytes 6030164 | solution.py:108
  731.0 14.8 %collective-permute-done.1 = f32[128,128]{1,0:T(8,128)S(1)} collective-permute-done((f32[128,128]{1,0:T(8,128)S(1)}, f32[128,128]{1,0:T(8,128)S(1)}, u32[]{:S(2)}, u32[]{:S(2)}) %collective-permute-start.1) | collective-permute-done | bytes 65568 | tf_op jit(solution)/shard_map/while/body/eval_jaxpr/ppermute | solution.py:15
  745.8 20.8 %collective-permute-start = (f32[128,128]{1,0:T(8,128)S(1)}, f32[128,128]{1,0:T(8,128)S(1)}, u32[]{:S(2)}, u32[]{:S(2)}) collective-permute-start(f32[128,128]{1,0:T(8,128)S(1)} %slice.171), channel_id=1, source_target_pairs={{8,0},{16,8},{24,16},{9,1},{17,9},{25,17},{10,2},{18,10},{26,18},{... | collective-permute-start | bytes 196616 | tf_op jit(solution)/shard_map/while/body/eval_jaxpr/ppermute | solution.py:15
  768.8 18.7 %collective-permute-done.1 = f32[128,128]{1,0:T(8,128)S(1)} collective-permute-done((f32[128,128]{1,0:T(8,128)S(1)}, f32[128,128]{1,0:T(8,128)S(1)}, u32[]{:S(2)}, u32[]{:S(2)}) %collective-permute-start.1) | collective-permute-done | bytes 65568 | tf_op jit(solution)/shard_map/while/body/eval_jaxpr/ppermute | solution.py:15
  793.3 16.3 %conditional.2 = (f32[2048,128]{1,0:T(8,128)S(1)}, f32[128,128]{1,0:T(8,128)S(1)}) conditional(s32[]{:T(128)} %convert_element_type.11, f32[2048,128]{1,0:T(8,128)S(1)} %get-tuple-element.370, (s32[]{:T(128)}, f32[2048,128]{1,0:T(8,128)S(1)}, f32[128,128]{1,0:T(8,128)S(1)}, s32[]{:T(128)}, s32[1,4,3]{1,0,2:T(1,128)S(1)}, ...), branch_computations={%region_33.33_spmd, %region_34.34_spmd} | conditional | flops 503545856 | bytes 5374306 | solution.py:89
  820.0 18.7 %collective-permute-done.1 = f32[128,128]{1,0:T(8,128)S(1)} collective-permute-done((f32[128,128]{1,0:T(8,128)S(1)}, f32[128,128]{1,0:T(8,128)S(1)}, u32[]{:S(2)}, u32[]{:S(2)}) %collective-permute-start.1) | collective-permute-done | bytes 65568 | tf_op jit(solution)/shard_map/while/body/eval_jaxpr/ppermute | solution.py:15
  844.4 16.2 %conditional.2 = (f32[2048,128]{1,0:T(8,128)S(1)}, f32[128,128]{1,0:T(8,128)S(1)}) conditional(s32[]{:T(128)} %convert_element_type.11, f32[2048,128]{1,0:T(8,128)S(1)} %get-tuple-element.370, (s32[]{:T(128)}, f32[2048,128]{1,0:T(8,128)S(1)}, f32[128,128]{1,0:T(8,128)S(1)}, s32[]{:T(128)}, s32[1,4,3]{1,0,2:T(1,128)S(1)}, ...), branch_computations={%region_33.33_spmd, %region_34.34_spmd} | conditional | flops 503545856 | bytes 5374306 | solution.py:89
  871.4 18.7 %collective-permute-done.1 = f32[128,128]{1,0:T(8,128)S(1)} collective-permute-done((f32[128,128]{1,0:T(8,128)S(1)}, f32[128,128]{1,0:T(8,128)S(1)}, u32[]{:S(2)}, u32[]{:S(2)}) %collective-permute-start.1) | collective-permute-done | bytes 65568 | tf_op jit(solution)/shard_map/while/body/eval_jaxpr/ppermute | solution.py:15
  895.8 16.3 %conditional.2 = (f32[2048,128]{1,0:T(8,128)S(1)}, f32[128,128]{1,0:T(8,128)S(1)}) conditional(s32[]{:T(128)} %convert_element_type.11, f32[2048,128]{1,0:T(8,128)S(1)} %get-tuple-element.370, (s32[]{:T(128)}, f32[2048,128]{1,0:T(8,128)S(1)}, f32[128,128]{1,0:T(8,128)S(1)}, s32[]{:T(128)}, s32[1,4,3]{1,0,2:T(1,128)S(1)}, ...), branch_computations={%region_33.33_spmd, %region_34.34_spmd} | conditional | flops 503545856 | bytes 5374306 | solution.py:89
  922.9 18.7 %collective-permute-done.1 = f32[128,128]{1,0:T(8,128)S(1)} collective-permute-done((f32[128,128]{1,0:T(8,128)S(1)}, f32[128,128]{1,0:T(8,128)S(1)}, u32[]{:S(2)}, u32[]{:S(2)}) %collective-permute-start.1) | collective-permute-done | bytes 65568 | tf_op jit(solution)/shard_map/while/body/eval_jaxpr/ppermute | solution.py:15
  947.3 16.2 %conditional.2 = (f32[2048,128]{1,0:T(8,128)S(1)}, f32[128,128]{1,0:T(8,128)S(1)}) conditional(s32[]{:T(128)} %convert_element_type.11, f32[2048,128]{1,0:T(8,128)S(1)} %get-tuple-element.370, (s32[]{:T(128)}, f32[2048,128]{1,0:T(8,128)S(1)}, f32[128,128]{1,0:T(8,128)S(1)}, s32[]{:T(128)}, s32[1,4,3]{1,0,2:T(1,128)S(1)}, ...), branch_computations={%region_33.33_spmd, %region_34.34_spmd} | conditional | flops 503545856 | bytes 5374306 | solution.py:89
  (259 shorter events, 172.8 us)
Async XLA Ops:
  6.5 475.6 %all-gather.49.cloned.1.call-start = ((), (), s32[]{:S(2)}) async-start(), calls=%async_computation | async-start | bytes 1179648 | tf_op jit(solution)/shard_map/all_gather | solution.py:9
  26.4 458.0 %all-gather.51.cloned.1.call-start = ((), (), s32[]{:S(2)}) async-start(), calls=%async_computation.1 | async-start | bytes 1179648 | tf_op jit(solution)/shard_map/all_gather | solution.py:9
  27.2 458.6 %all-gather.53.cloned.1.call-start = ((), (), s32[]{:S(2)}) async-start(), calls=%async_computation.2 | async-start | bytes 1179648 | tf_op jit(solution)/shard_map/all_gather | solution.py:9
  27.9 459.2 %all-gather.55.cloned.1.call-start = ((), (), s32[]{:S(2)}) async-start(), calls=%async_computation.3 | async-start | bytes 1179648 | tf_op jit(solution)/shard_map/all_gather | solution.py:9
  28.5 460.0 %all-gather.57.cloned.1.call-start = ((), (), s32[]{:S(2)}) async-start(), calls=%async_computation.4 | async-start | bytes 1179648 | tf_op jit(solution)/shard_map/all_gather | solution.py:9
  29.1 460.7 %all-gather.59.cloned.1.call-start = ((), (), s32[]{:S(2)}) async-start(), calls=%async_computation.5 | async-start | bytes 1179648 | tf_op jit(solution)/shard_map/all_gather | solution.py:9
  29.7 461.5 %all-gather.61.cloned.1.call-start = ((), (), s32[]{:S(2)}) async-start(), calls=%async_computation.6 | async-start | bytes 1179648 | tf_op jit(solution)/shard_map/all_gather | solution.py:9
  53.5 439.0 %all-gather.63.cloned.1.call-start = ((), (), s32[]{:S(2)}) async-start(), calls=%async_computation.7 | async-start | bytes 1179648 | tf_op jit(solution)/shard_map/all_gather | solution.py:9
  54.2 439.6 %all-gather.65.cloned.1.call-start = ((), (), s32[]{:S(2)}) async-start(), calls=%async_computation.8 | async-start | bytes 1179648 | tf_op jit(solution)/shard_map/all_gather | solution.py:9
  54.9 440.2 %all-gather.67.cloned.1.call-start = ((), (), s32[]{:S(2)}) async-start(), calls=%async_computation.9 | async-start | bytes 1179648 | tf_op jit(solution)/shard_map/all_gather | solution.py:9
  55.5 451.3 %all-gather.69.cloned.1.call-start = ((), (), s32[]{:S(2)}) async-start(), calls=%async_computation.10 | async-start | bytes 1179648 | tf_op jit(solution)/shard_map/all_gather | solution.py:9
  56.3 491.9 %all-gather.71.cloned.1.call-start = ((), (), s32[]{:S(2)}) async-start(), calls=%async_computation.11 | async-start | bytes 1179648 | tf_op jit(solution)/shard_map/all_gather | solution.py:9
  56.8 533.9 %all-gather.73.cloned.1.call-start = ((), (), s32[]{:S(2)}) async-start(), calls=%async_computation.12 | async-start | bytes 1179648 | tf_op jit(solution)/shard_map/all_gather | solution.py:9
  57.6 574.2 %all-gather.75.cloned.1.call-start = ((), (), s32[]{:S(2)}) async-start(), calls=%async_computation.13 | async-start | bytes 1179648 | tf_op jit(solution)/shard_map/all_gather | solution.py:9
  58.2 614.6 %all-gather.77.cloned.1.call-start = ((), (), s32[]{:S(2)}) async-start(), calls=%async_computation.14 | async-start | bytes 1179648 | tf_op jit(solution)/shard_map/all_gather | solution.py:9
  58.8 655.0 %all-gather.79.cloned.1.call-start = ((), (), s32[]{:S(2)}) async-start(), calls=%async_computation.15 | async-start | bytes 1179648 | tf_op jit(solution)/shard_map/all_gather | solution.py:9
  715.1 5.2 collective-permute-start
  720.3 3.7 collective-permute-start.1
  724.0 5.8 collective-permute-start
  729.8 16.1 %collective-permute-start.1 = (f32[128,128]{1,0:T(8,128)S(1)}, f32[128,128]{1,0:T(8,128)S(1)}, u32[]{:S(2)}, u32[]{:S(2)}) collective-permute-start(f32[128,128]{1,0:T(8,128)S(1)} %get-tuple-element.352), channel_id=1, source_target_pairs={{0,8},{8,16},{16,24},{1,9},{9,17},{17,25},{2,10},{10,18},{18,26},{... | collective-permute-start | bytes 196616 | tf_op jit(solution)/shard_map/while/body/eval_jaxpr/ppermute | solution.py:15
  745.8 21.7 %collective-permute-start = (f32[128,128]{1,0:T(8,128)S(1)}, f32[128,128]{1,0:T(8,128)S(1)}, u32[]{:S(2)}, u32[]{:S(2)}) collective-permute-start(f32[128,128]{1,0:T(8,128)S(1)} %slice.171), channel_id=1, source_target_pairs={{8,0},{16,8},{24,16},{9,1},{17,9},{25,17},{10,2},{18,10},{26,18},{... | collective-permute-start | bytes 196616 | tf_op jit(solution)/shard_map/while/body/eval_jaxpr/ppermute | solution.py:15
  767.5 20.0 %collective-permute-start.1 = (f32[128,128]{1,0:T(8,128)S(1)}, f32[128,128]{1,0:T(8,128)S(1)}, u32[]{:S(2)}, u32[]{:S(2)}) collective-permute-start(f32[128,128]{1,0:T(8,128)S(1)} %get-tuple-element.352), channel_id=1, source_target_pairs={{0,8},{8,16},{16,24},{1,9},{9,17},{17,25},{2,10},{10,18},{18,26},{... | collective-permute-start | bytes 196616 | tf_op jit(solution)/shard_map/while/body/eval_jaxpr/ppermute | solution.py:15
  787.5 5.7 collective-permute-start
  812.7 6.0 collective-permute-start
  818.7 20.0 %collective-permute-start.1 = (f32[128,128]{1,0:T(8,128)S(1)}, f32[128,128]{1,0:T(8,128)S(1)}, u32[]{:S(2)}, u32[]{:S(2)}) collective-permute-start(f32[128,128]{1,0:T(8,128)S(1)} %get-tuple-element.352), channel_id=1, source_target_pairs={{0,8},{8,16},{16,24},{1,9},{9,17},{17,25},{2,10},{10,18},{18,26},{... | collective-permute-start | bytes 196616 | tf_op jit(solution)/shard_map/while/body/eval_jaxpr/ppermute | solution.py:15
  838.7 5.7 collective-permute-start
  863.8 6.3 collective-permute-start
  870.1 20.0 %collective-permute-start.1 = (f32[128,128]{1,0:T(8,128)S(1)}, f32[128,128]{1,0:T(8,128)S(1)}, u32[]{:S(2)}, u32[]{:S(2)}) collective-permute-start(f32[128,128]{1,0:T(8,128)S(1)} %get-tuple-element.352), channel_id=1, source_target_pairs={{0,8},{8,16},{16,24},{1,9},{9,17},{17,25},{2,10},{10,18},{18,26},{... | collective-permute-start | bytes 196616 | tf_op jit(solution)/shard_map/while/body/eval_jaxpr/ppermute | solution.py:15
  890.1 5.7 collective-permute-start
  915.3 6.3 collective-permute-start
  921.6 20.0 %collective-permute-start.1 = (f32[128,128]{1,0:T(8,128)S(1)}, f32[128,128]{1,0:T(8,128)S(1)}, u32[]{:S(2)}, u32[]{:S(2)}) collective-permute-start(f32[128,128]{1,0:T(8,128)S(1)} %get-tuple-element.352), channel_id=1, source_target_pairs={{0,8},{8,16},{16,24},{1,9},{9,17},{17,25},{2,10},{10,18},{18,26},{... | collective-permute-start | bytes 196616 | tf_op jit(solution)/shard_map/while/body/eval_jaxpr/ppermute | solution.py:15
  941.6 5.7 collective-permute-start
  (11 other events, 144.7 us)
Sparse Core Ops, SparseCore 0:
  26.5 40.5 all-gather.48
  69.2 41.8 all-gather.50
  113.2 42.7 all-gather.52
  158.0 41.1 all-gather.54
  201.2 42.9 all-gather.56
  246.1 42.7 all-gather.58
  291.0 42.4 all-gather.60
  335.7 39.1 all-gather.62
  377.0 43.6 all-gather.64
  422.7 41.4 all-gather.66
  466.3 40.4 all-gather.68
  508.8 39.3 all-gather.70
  550.3 40.4 all-gather.72
  592.7 38.9 all-gather.74
  633.7 38.9 all-gather.76
  674.7 38.9 all-gather.78
